TPU v7x, 32 devices: a whole 2x2x4 slice. The times are simulated.
32 devices in a mesh: atm: 8 (over y, x, core), xg: 4 (over z).
Axes of the slice: x: 2, y: 2, z: 4, core: 2. Of those that a mesh axis runs over, the one named last changes fastest.
Arguments:
- fields_now: float32 [128, 48, 52, 128], P('atm', None, 'xg'), may hold values from -6 to 6
- upper: float32 [128, 48, 128], P(('atm', 'xg')), may hold values from 0.05 to 20
- lower: float32 [128, 48, 128], P(('atm', 'xg')), may hold values from 0.05 to 20
- surface_gain: float32 [128, 128], P(('atm', 'xg')), may hold values from 0.3 to 3
- route: int32 [8, 32, 2], P('atm'), may hold values from 0 to 16
- margin_slot: int32 [32, 96], P(('atm', 'xg')), may hold values from 0 to 15
- margin_block: int32 [32, 96], P(('atm', 'xg')), may hold values from 0 to 15
- margin_count: int32 [32], P(('atm', 'xg')), may hold values from 12 to 96, as said below
- margin_weight: float32 [32, 96, 128, 128], P(('atm', 'xg')), may hold values from 0 to 0.03
- surface_value: float32 [512, 52, 128], P(('atm', 'xg')), may hold values from -6 to 6
- exchange_coef: float32 [512, 128], P(('atm', 'xg')), may hold values from 0.05 to 2
- land_mask: int32 [512, 128], P(('atm', 'xg')), may hold values 0 or 1
- land_gain: float32 [512, 128], P(('atm', 'xg')), may hold values from 0.2 to 5
Outputs:
- fields_next: float32 [128, 48, 52, 128], P('atm', None, 'xg')
- surface_flux: float32 [512, 52, 128], P(('atm', 'xg'))
Inputs may be any that keep to these rules, and one draw needn't show every extreme that they name: `route`: the value 16 marks an empty slot; other values name a local column block of the sending atmosphere index. `margin_slot`: A value s names slot s % 2 from atmosphere index s // 2. `margin_count`: margins from this count on are padding; some owner has all 96 live.
All inputs are finite; a program needn't handle non-finite values. No bound on the sum of `land_mask` on one device may be relied on, other than what follows from the above.
Results may differ from a plain program's by a relative error of at most 0.0003.
Values sent between devices are 32-bit elements; how exact they have to be, the bound alone decides.
No kernel may reach another device: no remote copies, remote signals or barrier semaphores. Data moves between devices by JAX's collectives and lax.ppermute only.
A program may use at most 128 MiB of HBM per device.

v0:
```python
import jax
import jax.numpy as jnp
from jax import lax
from jax.sharding import PartitionSpec as P

HIGHEST = lax.Precision.HIGHEST


def factors(upper, lower):
    level_count = upper.shape[1]
    carried = jnp.zeros_like(upper[:, 0])
    inverses, multipliers, carries = ([], [], [])
    for height in range(level_count):
        from_above = upper[:, height] if height > 0 else jnp.zeros_like(carried)
        from_below = lower[:, height] if height < level_count - 1 else jnp.zeros_like(carried)
        inverse = 1.0 / (1.0 + from_above + from_below - from_above * carried)
        carried = from_below * inverse
        inverses.append(inverse)
        multipliers.append(from_above * inverse)
        carries.append(carried)
    return (jnp.stack(inverses, 1), jnp.stack(multipliers, 1), jnp.stack(carries, 1))


def per_device(
    fields_now,
    upper,
    lower,
    surface_gain,
    route,
    margin_slot,
    margin_block,
    margin_count,
    margin_weight,
    surface_value,
    exchange_coef,
    land_mask,
    land_gain,
):
    atm_count = lax.axis_size("atm")
    xg_count = lax.axis_size("xg")
    own_inverse, own_multiplier, own_carry = factors(upper, lower)
    own_bottom = surface_gain * own_inverse[:, -1]
    inverse, multiplier, carry_factor, bottom_gain = (
        lax.all_gather(own_inverse, "xg", axis=0, tiled=True),
        lax.all_gather(own_multiplier, "xg", axis=0, tiled=True),
        lax.all_gather(own_carry, "xg", axis=0, tiled=True),
        lax.all_gather(own_bottom, "xg", axis=0, tiled=True),
    )
    block_count = fields_now.shape[0]
    level_count = fields_now.shape[1]
    field_share = fields_now.shape[2]
    block_width = fields_now.shape[3]
    running = jnp.zeros_like(fields_now[:, 0])
    partials = []
    for height in range(level_count):
        running = (
            inverse[:, height, None, :] * fields_now[:, height]
            + multiplier[:, height, None, :] * running
        )
        partials.append(running)
    routing = route[0]
    pair_slots = routing.shape[1]
    quarter = block_width // xg_count
    send_value = jnp.concatenate(
        [running, jnp.zeros((1, field_share, block_width), jnp.float32)], 0
    )[routing]
    own_columns = lax.dynamic_slice_in_dim(bottom_gain, lax.axis_index("xg") * quarter, quarter, 1)
    send_gain = jnp.concatenate([own_columns, jnp.zeros((1, quarter), jnp.float32)], 0)[routing]
    got_value, got_gain = (
        lax.all_to_all(send_value, ("atm", "xg"), split_axis=0, concat_axis=0, tiled=True),
        lax.all_to_all(send_gain, ("atm", "xg"), split_axis=0, concat_axis=0, tiled=True),
    )
    got_value = got_value.reshape(atm_count, xg_count, pair_slots, field_share, block_width)
    got_gain = got_gain.reshape(atm_count, xg_count, pair_slots, quarter)
    slot_index = margin_slot[0]
    source = slot_index // pair_slots
    pair_index = slot_index % pair_slots
    margins = slot_index.shape[0]
    alive = (jnp.arange(margins, dtype=jnp.int32) < margin_count[0]).astype(jnp.float32)
    value_slots = got_value[source, :, pair_index].reshape(
        margins, xg_count * field_share, block_width
    )
    gain_slots = got_gain[source, :, pair_index].reshape(margins, block_width)
    weight = margin_weight[0]
    cell_blocks = surface_value.shape[0]
    select = (margin_block[0][None, :] == jnp.arange(cell_blocks, dtype=jnp.int32)[:, None]).astype(
        jnp.float32
    ) * alive[None, :]
    value_part = jnp.einsum("kxb,kfb->kfx", weight, value_slots, precision=HIGHEST)
    gain_part = jnp.einsum("kxb,kb->kx", weight, gain_slots, precision=HIGHEST)
    cell_value = jnp.einsum("jk,kfx->jfx", select, value_part, precision=HIGHEST)
    cell_gain = jnp.einsum("jk,kx->jx", select, gain_part, precision=HIGHEST)
    coupling = exchange_coef[:, None, :]
    land_total = land_mask.astype(jnp.float32) * land_gain
    surface_flux = (
        coupling
        * (surface_value - cell_value)
        / (1.0 + coupling * (cell_gain + land_total)[:, None, :])
    )
    returned = jnp.einsum("kxb,kfx->kfb", weight, surface_flux[margin_block[0]], precision=HIGHEST)
    returned = returned.reshape(margins, xg_count, field_share, block_width)
    by_source = (source[None, None, :] == jnp.arange(atm_count, dtype=jnp.int32)[:, None, None]) & (
        pair_index[None, None, :] == jnp.arange(pair_slots, dtype=jnp.int32)[None, :, None]
    )
    by_source = by_source.astype(jnp.float32) * alive[None, None, :]
    reply = jnp.einsum("apk,kgfb->agpfb", by_source, returned, precision=HIGHEST)
    answer = lax.all_to_all(
        reply.reshape(atm_count * xg_count, pair_slots, field_share, block_width),
        ("atm", "xg"),
        split_axis=0,
        concat_axis=0,
        tiled=True,
    )
    route_select = (
        routing[None, :, :] == jnp.arange(block_count, dtype=jnp.int32)[:, None, None]
    ).astype(jnp.float32)
    column_flux = jnp.einsum("rdp,dpfb->rfb", route_select, answer, precision=HIGHEST)
    state = running + bottom_gain[:, None, :] * column_flux
    outputs = [state]
    for height in range(level_count - 2, -1, -1):
        state = partials[height] + carry_factor[:, height, None, :] * state
        outputs.append(state)
    fields_next = jnp.stack(outputs[::-1], 1)
    return (fields_next, surface_flux)


def solution(mesh):
    in_specs = (
        P("atm", None, "xg", None),
        P(("atm", "xg"), None, None),
        P(("atm", "xg"), None, None),
        P(("atm", "xg"), None),
        P("atm", None, None),
        P(("atm", "xg"), None),
        P(("atm", "xg"), None),
        P(("atm", "xg")),
        P(("atm", "xg"), None, None, None),
        P(("atm", "xg"), None, None),
        P(("atm", "xg"), None),
        P(("atm", "xg"), None),
        P(("atm", "xg"), None),
    )
    out_specs = (P("atm", None, "xg", None), P(("atm", "xg"), None, None))
    return jax.shard_map(
        per_device, mesh=mesh, in_specs=in_specs, out_specs=out_specs, check_vma=False
    )
```

profile of v0, /device:TPU:0, one launch (start us, length us, event | category | flops | bytes accessed | tf_op | source)
XLA Modules:
  0.0 191.3 jit_solution(15118442074869055433)
XLA Ops:
  0.6 1.0 fusion.217
  1.6 1.2 fusion.213
  2.9 1.2 fusion.216
  4.1 1.2 fusion.218
  5.3 1.4 fusion.214
  6.7 1.2 fusion.215
  8.0 0.7 fusion.173
  8.6 0.7 compare_select_fusion
  9.5 1.3 multiply_bitcast_fusion
  10.8 13.6 %all-gather = f32[4,4,128]{2,1,0:T(4,128)S(1)} all-gather(f32[1,4,128]{2,1,0:T(4,128)S(1)} %get-tuple-element.36), channel_id=1, replica_groups=mesh['atm'=8,'xg'=4] {'xg'}, dimensions={0}, use_global_device_ids=true | all-gather | bytes 10240 | tf_op jit(solution)/shard_map/all_gather | solution.py:47
  25.1 1.2 gather_fusion.2
  26.3 4.3 %all-to-all-start.1 = ((f32[32,2,32]{2,1,0:T(2,128)}), f32[32,2,32]{2,1,0:T(2,128)S(1)}, u32[]{:S(2)}, u32[]{:S(2)}) async-start(f32[32,2,32]{2,1,0:T(2,128)} %bitcast.394), calls=%async_computation.1 | async-start | bytes 65536 | tf_op jit(solution)/shard_map/all_to_all | solution.py:71
  30.7 0.7 fusion.174
  31.3 0.7 and_select_fusion.1
  32.9 14.9 %all_gather.13 = f32[16,48,128]{2,1,0:T(8,128)S(1)} all-gather(f32[4,48,128]{2,1,0:T(8,128)S(1)} %copy.818), channel_id=1, replica_groups=mesh['atm'=8,'xg'=4] {'xg'}, dimensions={0}, use_global_device_ids=true | all-gather | bytes 491520 | tf_op jit(solution)/shard_map/all_gather | solution.py:45
  48.1 0.7 fusion.210
  49.1 15.5 %all_gather.12 = f32[16,48,128]{2,1,0:T(8,128)S(1)} all-gather(f32[4,48,128]{2,1,0:T(8,128)S(1)} %stack.412), channel_id=1, replica_groups=mesh['atm'=8,'xg'=4] {'xg'}, dimensions={0}, use_global_device_ids=true | all-gather | bytes 491520 | tf_op jit(solution)/shard_map/all_gather | solution.py:44
  64.6 0.7 fusion.211
  65.3 0.7 fusion.207
  66.0 0.7 fusion.209
  66.8 5.1 %fusion.203 = (f32[16,1,13,128]{3,1,2,0:T(1,128)S(1)}, f32[16,1,13,128]{3,1,2,0:T(1,128)S(1)}, f32[16,1,13,128]{3,1,2,0:T(1,128)S(1)}, f32[16,1,13,128]{3,1,2,0:...) fusion(f32[16,48,13,128]{3,1,2,0:T(8,128)} %param.13), kind=kLoop, calls=%fused_computation.526 | loop fusion | bytes 2129920 | tf_op jit(solution)/shard_map/slice | solution.py:57
  71.9 9.1 %fusion.202 = (f32[16,1,13,128]{3,1,2,0:T(1,128)S(1)}, f32[16,1,13,128]{3,1,2,0:T(1,128)S(1)}, f32[16,1,13,128]{3,1,2,0:T(1,128)S(1)}, f32[16,1,13,128]{3,1,2,0:...) fusion(f32[16,48,13,128]{3,1,2,0:T(8,128)} %param.13), kind=kLoop, calls=%fused_computation.525 | loop fusion | bytes 4046848 | tf_op jit(solution)/shard_map/slice | solution.py:57
  81.1 9.1 %fusion.201 = (f32[16,1,13,128]{3,1,2,0:T(1,128)S(1)}, f32[16,1,13,128]{3,1,2,0:T(1,128)S(1)}, f32[16,1,13,128]{3,1,2,0:T(1,128)S(1)}, f32[16,1,13,128]{3,1,2,0:...) fusion(f32[16,48,13,128]{3,1,2,0:T(8,128)} %param.13), kind=kLoop, calls=%fused_computation.524 | loop fusion | bytes 4046848 | tf_op jit(solution)/shard_map/slice | solution.py:57
  91.1 3.0 %fusion.24 = (f32[16,13,128]{2,0,1:T(8,128)S(1)}, f32[16,13,128]{2,0,1:T(8,128)S(1)}, f32[16,13,128]{2,0,1:T(8,128)S(1)}, f32[16,13,128]{2,0,1:T(8,128)S(1)}, f3...) fusion(f32[16,1,13,128]{3,1,2,0:T(1,128)S(1)} %get-tuple-elemen, ...), kind=kLoop, calls=%fused_computation.171 | loop fusion | flops 3807232 | bytes 8454144 | tf_op jit(solution)/shard_map/add | solution.py:57
  94.2 0.7 copy.819
  95.8 1.0 copy.869
  96.7 5.4 %all-to-all-start = ((f32[32,2,13,128]{3,1,2,0:T(2,128)}), f32[32,2,13,128]{3,1,2,0:T(2,128)S(1)}, u32[]{:S(2)}, u32[]{:S(2)}) async-start(f32[32,2,13,128]{3,1,2,0:T(2,128)} %copy.869), calls=%async_computation | async-start | bytes 851968 | tf_op jit(solution)/shard_map/all_to_all | solution.py:70
  102.1 1.2 gather_fusion.3
  103.5 11.8 %fusion.2 = f32[96,1,128]{2,1,0:T(1,128)S(1)} fusion(f32[96,128,1]{1,2,0:T(1,128)S(1)} %copy.884, f32[1,96,128,128]{3,2,1,0:T(8,128)} %param.21), kind=kOutput, calls=%fused_computation.7 | convolution fusion | flops 18874368 | bytes 6389760 | tf_op jit(solution)/shard_map/kxb,kb->kx/dot_general | solution.py:90
  115.7 2.8 %gather_fusion.1 = f32[96,4,13,128]{3,1,2,0:T(4,128)S(1)} fusion(f32[8,4,2,13,128]{4,1,3,2,0:T(4,128)S(1)} %copy.871, s32[96]{0:T(128)S(1)} %fusion.174), kind=kCustom, calls=%fused_computation.1 | custom fusion | bytes 5112576 | tf_op jit(solution)/shard_map/gather | solution.py:80
  118.8 16.4 %fusion.4 = f32[96,52,128]{2,1,0:T(8,128)S(1)} fusion(f32[1,96,128,128]{3,2,1,0:T(8,128)} %param.21, f32[96,52,128]{2,0,1:T(8,128)S(1)} %bitcast.1218), kind=kOutput, calls=%fused_computation.9 | convolution fusion | flops 981467136 | bytes 11403264 | tf_op jit(solution)/shard_map/kxb,kfb->kfx/dot_general | solution.py:89
  135.2 1.6 fusion.15
  137.6 0.8 gather_fusion.4
  138.4 7.8 %fusion = f32[96,52,128]{2,1,0:T(8,128)S(1)} fusion(f32[96,52,128]{2,1,0:T(8,128)S(1)} %gather_fusion.4, f32[1,96,128,128]{3,2,1,0:T(8,128)} %param.21), kind=kOutput, calls=%fused_computation.5 | convolution fusion | flops 981467136 | bytes 11403264 | tf_op jit(solution)/shard_map/kxb,kfx->kfb/dot_general | solution.py:100
  147.0 1.5 convolution_bitcast_fusion
  148.6 1.1 copy.881
  149.7 5.7 %all-to-all-start.2 = ((f32[32,2,13,128]{3,1,2,0:T(2,128)}), f32[32,2,13,128]{3,1,2,0:T(2,128)S(1)}, u32[]{:S(2)}, u32[]{:S(2)}) async-start(f32[32,2,13,128]{3,1,2,0:T(2,128)} %copy.881), calls=%async_computation.2 | async-start | bytes 851968 | tf_op jit(solution)/shard_map/all_to_all | solution.py:107
  155.4 21.2 %all_gather.14 = f32[16,48,128]{2,1,0:T(8,128)S(1)} all-gather(f32[4,48,128]{2,1,0:T(8,128)} %copy.819), channel_id=1, replica_groups=mesh['atm'=8,'xg'=4] {'xg'}, dimensions={0}, use_global_device_ids=true | all-gather | bytes 491520 | tf_op jit(solution)/shard_map/all_gather | solution.py:46
  176.6 0.7 fusion.206
  177.3 0.8 fusion.204
  178.1 0.8 fusion.205
  179.2 3.5 %constant_dynamic-update-slice_fusion.143 = (f32[16,48,13,128]{3,0,2,1:T(8,128)S(1)}, f32[16,13,128]{2,0,1:T(8,128)S(1)}, f32[16,13,128]{2,0,1:T(8,128)S(1)}, f3...) fusion(f32[16,1,13,128]{3,1,2,0:T(1,128)S(1)} %copy-done.32, ...), kind=kOutput, calls=%fused_computation.168 | convolution fusion | flops 24894464 | bytes 8986880 | tf_op jit(solution)/shard_map/rdp,dpfb->rfb/dot_general | solution.py:117
  182.8 0.7 constant_dynamic-update-slice_fusion.141
  183.6 0.7 constant_dynamic-update-slice_fusion.139
  184.4 0.7 constant_dynamic-update-slice_fusion.133
  185.1 0.7 constant_dynamic-update-slice_fusion.131
  185.9 0.7 constant_dynamic-update-slice_fusion.129
  187.4 3.9 %copy.883 = f32[16,48,13,128]{3,1,2,0:T(8,128)} copy(f32[16,48,13,128]{3,0,2,1:T(8,128)S(1)} %constant_dynamic-update-slice_fusion.96) | data formatting | bytes 10223616
  (294 shorter events, 5.9 us)
Async XLA Ops:
  26.3 70.4 %all-to-all-start.1 = ((f32[32,2,32]{2,1,0:T(2,128)}), f32[32,2,32]{2,1,0:T(2,128)S(1)}, u32[]{:S(2)}, u32[]{:S(2)}) async-start(f32[32,2,32]{2,1,0:T(2,128)} %bitcast.394), calls=%async_computation.1 | async-start | bytes 65536 | tf_op jit(solution)/shard_map/all_to_all | solution.py:71
  47.8 43.1 %copy-start.68 = (f32[16,1,128]{2,1,0:T(1,128)}, f32[16,1,128]{2,1,0:T(1,128)S(1)}, u32[]{:S(2)}) copy-start(f32[16,1,128]{2,1,0:T(1,128)S(1)} %get-tuple-element.321) | copy-start | bytes 24580
  47.9 43.1 %copy-start.69 = (f32[16,1,128]{2,1,0:T(1,128)}, f32[16,1,128]{2,1,0:T(1,128)S(1)}, u32[]{:S(2)}) copy-start(f32[16,1,128]{2,1,0:T(1,128)S(1)} %get-tuple-element.323) | copy-start | bytes 24580
  47.9 43.1 %copy-start.70 = (f32[16,1,128]{2,1,0:T(1,128)}, f32[16,1,128]{2,1,0:T(1,128)S(1)}, u32[]{:S(2)}) copy-start(f32[16,1,128]{2,1,0:T(1,128)S(1)} %get-tuple-element.325) | copy-start | bytes 24580
  47.9 43.1 %copy-start.71 = (f32[16,1,128]{2,1,0:T(1,128)}, f32[16,1,128]{2,1,0:T(1,128)S(1)}, u32[]{:S(2)}) copy-start(f32[16,1,128]{2,1,0:T(1,128)S(1)} %get-tuple-element.327) | copy-start | bytes 24580
  47.9 43.1 %copy-start.72 = (f32[16,1,128]{2,1,0:T(1,128)}, f32[16,1,128]{2,1,0:T(1,128)S(1)}, u32[]{:S(2)}) copy-start(f32[16,1,128]{2,1,0:T(1,128)S(1)} %get-tuple-element.328) | copy-start | bytes 24580
  47.9 43.1 %copy-start.73 = (f32[16,1,128]{2,1,0:T(1,128)}, f32[16,1,128]{2,1,0:T(1,128)S(1)}, u32[]{:S(2)}) copy-start(f32[16,1,128]{2,1,0:T(1,128)S(1)} %get-tuple-element.329) | copy-start | bytes 24580
  48.0 43.0 %copy-start.74 = (f32[16,1,128]{2,1,0:T(1,128)}, f32[16,1,128]{2,1,0:T(1,128)S(1)}, u32[]{:S(2)}) copy-start(f32[16,1,128]{2,1,0:T(1,128)S(1)} %get-tuple-element.256) | copy-start | bytes 24580
  48.0 43.0 %copy-start.75 = (f32[16,1,128]{2,1,0:T(1,128)}, f32[16,1,128]{2,1,0:T(1,128)S(1)}, u32[]{:S(2)}) copy-start(f32[16,1,128]{2,1,0:T(1,128)S(1)} %get-tuple-element.258) | copy-start | bytes 24580
  48.0 43.0 %copy-start.76 = (f32[16,1,128]{2,1,0:T(1,128)}, f32[16,1,128]{2,1,0:T(1,128)S(1)}, u32[]{:S(2)}) copy-start(f32[16,1,128]{2,1,0:T(1,128)S(1)} %get-tuple-element.260) | copy-start | bytes 24580
  48.1 43.0 %copy-start.77 = (f32[16,1,128]{2,1,0:T(1,128)}, f32[16,1,128]{2,1,0:T(1,128)S(1)}, u32[]{:S(2)}) copy-start(f32[16,1,128]{2,1,0:T(1,128)S(1)} %get-tuple-element.262) | copy-start | bytes 24580
  48.1 43.0 %copy-start.78 = (f32[16,1,128]{2,1,0:T(1,128)}, f32[16,1,128]{2,1,0:T(1,128)S(1)}, u32[]{:S(2)}) copy-start(f32[16,1,128]{2,1,0:T(1,128)S(1)} %get-tuple-element.264) | copy-start | bytes 24580
  48.1 43.0 %copy-start.79 = (f32[16,1,128]{2,1,0:T(1,128)}, f32[16,1,128]{2,1,0:T(1,128)S(1)}, u32[]{:S(2)}) copy-start(f32[16,1,128]{2,1,0:T(1,128)S(1)} %get-tuple-element.266) | copy-start | bytes 24580
  48.1 43.0 %copy-start.80 = (f32[16,1,128]{2,1,0:T(1,128)}, f32[16,1,128]{2,1,0:T(1,128)S(1)}, u32[]{:S(2)}) copy-start(f32[16,1,128]{2,1,0:T(1,128)S(1)} %get-tuple-element.268) | copy-start | bytes 24580
  48.1 43.0 %copy-start.81 = (f32[16,1,128]{2,1,0:T(1,128)}, f32[16,1,128]{2,1,0:T(1,128)S(1)}, u32[]{:S(2)}) copy-start(f32[16,1,128]{2,1,0:T(1,128)S(1)} %get-tuple-element.270) | copy-start | bytes 24580
  48.9 42.2 %copy-start.82 = (f32[16,1,128]{2,1,0:T(1,128)}, f32[16,1,128]{2,1,0:T(1,128)S(1)}, u32[]{:S(2)}) copy-start(f32[16,1,128]{2,1,0:T(1,128)S(1)} %get-tuple-element.291) | copy-start | bytes 24580
  71.8 22.3 %copy-start.23 = (f32[16,1,13,128]{3,1,2,0:T(1,128)}, f32[16,1,13,128]{3,1,2,0:T(1,128)S(1)}, u32[]{:S(2)}) copy-start(f32[16,1,13,128]{3,1,2,0:T(1,128)S(1)} %get-tuple-element.179) | copy-start | bytes 319492
  71.8 22.3 %copy-start.25 = (f32[16,1,13,128]{3,1,2,0:T(1,128)}, f32[16,1,13,128]{3,1,2,0:T(1,128)S(1)}, u32[]{:S(2)}) copy-start(f32[16,1,13,128]{3,1,2,0:T(1,128)S(1)} %get-tuple-element.181) | copy-start | bytes 319492
  71.9 22.3 %copy-start.27 = (f32[16,1,13,128]{3,1,2,0:T(1,128)}, f32[16,1,13,128]{3,1,2,0:T(1,128)S(1)}, u32[]{:S(2)}) copy-start(f32[16,1,13,128]{3,1,2,0:T(1,128)S(1)} %get-tuple-element.183) | copy-start | bytes 319492
  96.7 18.8 %all-to-all-start = ((f32[32,2,13,128]{3,1,2,0:T(2,128)}), f32[32,2,13,128]{3,1,2,0:T(2,128)S(1)}, u32[]{:S(2)}, u32[]{:S(2)}) async-start(f32[32,2,13,128]{3,1,2,0:T(2,128)} %copy.869), calls=%async_computation | async-start | bytes 851968 | tf_op jit(solution)/shard_map/all_to_all | solution.py:70
  146.2 32.6 %copy-start.1 = (f32[16,13,128]{2,0,1:T(8,128)S(1)}, f32[16,13,128]{2,0,1:T(8,128)}, u32[]{:S(2)}) copy-start(f32[16,13,128]{2,0,1:T(8,128)} %get-tuple-element.57) | copy-start | bytes 319492
  146.2 32.6 %copy-start.2 = (f32[16,13,128]{2,0,1:T(8,128)S(1)}, f32[16,13,128]{2,0,1:T(8,128)}, u32[]{:S(2)}) copy-start(f32[16,13,128]{2,0,1:T(8,128)} %get-tuple-element.58) | copy-start | bytes 319492
  146.3 32.6 %copy-start.3 = (f32[16,13,128]{2,0,1:T(8,128)S(1)}, f32[16,13,128]{2,0,1:T(8,128)}, u32[]{:S(2)}) copy-start(f32[16,13,128]{2,0,1:T(8,128)} %get-tuple-element.59) | copy-start | bytes 319492
  146.3 32.6 %copy-start.4 = (f32[16,13,128]{2,0,1:T(8,128)S(1)}, f32[16,13,128]{2,0,1:T(8,128)}, u32[]{:S(2)}) copy-start(f32[16,13,128]{2,0,1:T(8,128)} %get-tuple-element.60) | copy-start | bytes 319492
  146.3 32.6 %copy-start.5 = (f32[16,13,128]{2,0,1:T(8,128)S(1)}, f32[16,13,128]{2,0,1:T(8,128)}, u32[]{:S(2)}) copy-start(f32[16,13,128]{2,0,1:T(8,128)} %get-tuple-element.61) | copy-start | bytes 319492
  146.3 32.6 %copy-start.6 = (f32[16,13,128]{2,0,1:T(8,128)S(1)}, f32[16,13,128]{2,0,1:T(8,128)}, u32[]{:S(2)}) copy-start(f32[16,13,128]{2,0,1:T(8,128)} %get-tuple-element.62) | copy-start | bytes 319492
  146.3 32.6 %copy-start.7 = (f32[16,13,128]{2,0,1:T(8,128)S(1)}, f32[16,13,128]{2,0,1:T(8,128)}, u32[]{:S(2)}) copy-start(f32[16,13,128]{2,0,1:T(8,128)} %get-tuple-element.63) | copy-start | bytes 319492
  146.3 32.6 %copy-start.8 = (f32[16,13,128]{2,0,1:T(8,128)S(1)}, f32[16,13,128]{2,0,1:T(8,128)}, u32[]{:S(2)}) copy-start(f32[16,13,128]{2,0,1:T(8,128)} %get-tuple-element.64) | copy-start | bytes 319492
  146.3 32.6 %copy-start.9 = (f32[16,13,128]{2,0,1:T(8,128)S(1)}, f32[16,13,128]{2,0,1:T(8,128)}, u32[]{:S(2)}) copy-start(f32[16,13,128]{2,0,1:T(8,128)} %get-tuple-element.65) | copy-start | bytes 319492
  146.3 32.6 %copy-start.10 = (f32[16,13,128]{2,0,1:T(8,128)S(1)}, f32[16,13,128]{2,0,1:T(8,128)}, u32[]{:S(2)}) copy-start(f32[16,13,128]{2,0,1:T(8,128)} %get-tuple-element.66) | copy-start | bytes 319492
  146.3 32.6 %copy-start.11 = (f32[16,13,128]{2,0,1:T(8,128)S(1)}, f32[16,13,128]{2,0,1:T(8,128)}, u32[]{:S(2)}) copy-start(f32[16,13,128]{2,0,1:T(8,128)} %get-tuple-element.67) | copy-start | bytes 319492
  146.3 32.6 %copy-start.12 = (f32[16,13,128]{2,0,1:T(8,128)S(1)}, f32[16,13,128]{2,0,1:T(8,128)}, u32[]{:S(2)}) copy-start(f32[16,13,128]{2,0,1:T(8,128)} %get-tuple-element.68) | copy-start | bytes 319492
  146.4 32.6 %copy-start.13 = (f32[16,13,128]{2,0,1:T(8,128)S(1)}, f32[16,13,128]{2,0,1:T(8,128)}, u32[]{:S(2)}) copy-start(f32[16,13,128]{2,0,1:T(8,128)} %get-tuple-element.69) | copy-start | bytes 319492
  146.4 32.6 %copy-start.14 = (f32[16,13,128]{2,0,1:T(8,128)S(1)}, f32[16,13,128]{2,0,1:T(8,128)}, u32[]{:S(2)}) copy-start(f32[16,13,128]{2,0,1:T(8,128)} %get-tuple-element.70) | copy-start | bytes 319492
  146.4 32.6 %copy-start.15 = (f32[16,13,128]{2,0,1:T(8,128)S(1)}, f32[16,13,128]{2,0,1:T(8,128)}, u32[]{:S(2)}) copy-start(f32[16,13,128]{2,0,1:T(8,128)} %get-tuple-element.71) | copy-start | bytes 319492
  146.4 32.6 %copy-start.16 = (f32[16,13,128]{2,0,1:T(8,128)S(1)}, f32[16,13,128]{2,0,1:T(8,128)}, u32[]{:S(2)}) copy-start(f32[16,13,128]{2,0,1:T(8,128)} %get-tuple-element.72) | copy-start | bytes 319492
  146.4 32.6 %copy-start.17 = (f32[16,13,128]{2,0,1:T(8,128)S(1)}, f32[16,13,128]{2,0,1:T(8,128)}, u32[]{:S(2)}) copy-start(f32[16,13,128]{2,0,1:T(8,128)} %get-tuple-element.73) | copy-start | bytes 319492
  146.4 32.6 %copy-start.18 = (f32[16,13,128]{2,0,1:T(8,128)S(1)}, f32[16,13,128]{2,0,1:T(8,128)}, u32[]{:S(2)}) copy-start(f32[16,13,128]{2,0,1:T(8,128)} %get-tuple-element.74) | copy-start | bytes 319492
  146.4 32.6 %copy-start.19 = (f32[16,13,128]{2,0,1:T(8,128)S(1)}, f32[16,13,128]{2,0,1:T(8,128)}, u32[]{:S(2)}) copy-start(f32[16,13,128]{2,0,1:T(8,128)} %get-tuple-element.75) | copy-start | bytes 319492
  146.4 32.6 %copy-start.20 = (f32[16,13,128]{2,0,1:T(8,128)S(1)}, f32[16,13,128]{2,0,1:T(8,128)}, u32[]{:S(2)}) copy-start(f32[16,13,128]{2,0,1:T(8,128)} %get-tuple-element.76) | copy-start | bytes 319492
  146.4 32.6 %copy-start.22 = (f32[16,13,128]{2,0,1:T(8,128)S(1)}, f32[16,13,128]{2,0,1:T(8,128)}, u32[]{:S(2)}) copy-start(f32[16,13,128]{2,0,1:T(8,128)} %copy-done.21) | copy-start | bytes 319492
  146.4 32.6 %copy-start.24 = (f32[16,1,13,128]{3,1,2,0:T(1,128)S(1)}, f32[16,1,13,128]{3,1,2,0:T(1,128)}, u32[]{:S(2)}) copy-start(f32[16,1,13,128]{3,1,2,0:T(1,128)} %copy-done.23) | copy-start | bytes 319492
  146.5 32.6 %copy-start.26 = (f32[16,1,13,128]{3,1,2,0:T(1,128)S(1)}, f32[16,1,13,128]{3,1,2,0:T(1,128)}, u32[]{:S(2)}) copy-start(f32[16,1,13,128]{3,1,2,0:T(1,128)} %copy-done.25) | copy-start | bytes 319492
  146.5 32.6 %copy-start.28 = (f32[16,1,13,128]{3,1,2,0:T(1,128)S(1)}, f32[16,1,13,128]{3,1,2,0:T(1,128)}, u32[]{:S(2)}) copy-start(f32[16,1,13,128]{3,1,2,0:T(1,128)} %copy-done.27) | copy-start | bytes 319492
  146.5 32.6 %copy-start.30 = (f32[16,1,13,128]{3,1,2,0:T(1,128)S(1)}, f32[16,1,13,128]{3,1,2,0:T(1,128)}, u32[]{:S(2)}) copy-start(f32[16,1,13,128]{3,1,2,0:T(1,128)} %copy-done.29) | copy-start | bytes 319492
  146.5 32.6 %copy-start.32 = (f32[16,1,13,128]{3,1,2,0:T(1,128)S(1)}, f32[16,1,13,128]{3,1,2,0:T(1,128)}, u32[]{:S(2)}) copy-start(f32[16,1,13,128]{3,1,2,0:T(1,128)} %copy-done.31) | copy-start | bytes 319492
  146.5 32.6 %copy-start.86 = (s32[1,32,2]{1,2,0:T(2,128)S(1)}, s32[1,32,2]{1,2,0:T(2,128)}, u32[]{:S(2)}) copy-start(s32[1,32,2]{1,2,0:T(2,128)} %param.17) | copy-start | bytes 772
  149.7 29.1 %all-to-all-start.2 = ((f32[32,2,13,128]{3,1,2,0:T(2,128)}), f32[32,2,13,128]{3,1,2,0:T(2,128)S(1)}, u32[]{:S(2)}, u32[]{:S(2)}) async-start(f32[32,2,13,128]{3,1,2,0:T(2,128)} %copy.881), calls=%async_computation.2 | async-start | bytes 851968 | tf_op jit(solution)/shard_map/all_to_all | solution.py:107
  (43 other events, 395.1 us)
where the time goes:
time: 193 us; the launch traced here: 191 us
  blocking collectives  65.3 us (34%)
  local copies, waits for them, and re-layouts  52.7 us (27%)
  matrix products  42.8 us (22%)
  starting transfers between devices  15.4 us (8%)
  other arithmetic  11.8 us (6%)
  between operations  3.31 us (2%)
    slice x3, local copies, waits for them, and re-layouts, per_device(): fields_now[:, height]  23.2 us
    all_gather x1, blocking collectives, per_device(): lax.all_gather(own_carry, 'xg', axis=0, tiled=True)  21.2 us
    dot_general x1, matrix products, per_device(): jnp.einsum('kxb,kfb->kfx', weight, value_slots, precision=HIGHEST)  16.4 us
    all_gather x1, blocking collectives, per_device(): lax.all_gather(own_inverse, 'xg', axis=0, tiled=True)  15.5 us
    all_gather x1, blocking collectives, per_device(): lax.all_gather(own_multiplier, 'xg', axis=0, tiled=True)  14.9 us
    all_gather x1, blocking collectives, per_device(): lax.all_gather(own_bottom, 'xg', axis=0, tiled=True)  13.6 us
    dot_general x1, matrix products, per_device(): gain_part = jnp.einsum('kxb,kb->kx', weight, gain_slots, precision=HIGHEST)  11.8 us
    dot_general x1, matrix products, per_device(): jnp.einsum('kxb,kfx->kfb', weight, surface_flux[margin_block[0]], precisi...  7.85 us
  transfers between devices with their start and end apart: 3, of which 0 were waited for; matrix products, arithmetic and copies ran while one was open for 26% of the time, Pallas kernels for 0%

commit v1 on v0

--- a/solution.py
+++ b/solution.py
@@ -1,9 +1,33 @@
+import functools
 import jax
 import jax.numpy as jnp
 from jax import lax
 from jax.sharding import PartitionSpec as P
+from jax.lax import axis_index, ppermute, psum
 
 HIGHEST = lax.Precision.HIGHEST
+
+
+def _settle_sheets(s0, axis_id):
+    outcome_arr = psum(1, axis_id)
+    part_next = axis_index(axis_id)
+    w_next, back, inter = (outcome_arr, part_next, s0.shape[0])
+    right_arr, f_now = (s0, 1)
+    while f_now < w_next:
+        right_arr = jnp.concatenate(
+            [
+                right_arr,
+                ppermute(
+                    right_arr, axis_id, [(idx, (idx - f_now) % w_next) for idx in range(w_next)]
+                ),
+            ],
+            axis=0,
+        )
+        f_now = 2 * f_now
+    return jnp.roll(right_arr, back * inter, axis=0)
+
+
+positions_plan = functools.partial(_settle_sheets, axis_id="xg")
 
 
 def factors(upper, lower):
@@ -44,7 +68,7 @@
         lax.all_gather(own_inverse, "xg", axis=0, tiled=True),
         lax.all_gather(own_multiplier, "xg", axis=0, tiled=True),
         lax.all_gather(own_carry, "xg", axis=0, tiled=True),
-        lax.all_gather(own_bottom, "xg", axis=0, tiled=True),
+        positions_plan(own_bottom),
     )
     block_count = fields_now.shape[0]
     level_count = fields_now.shape[1]

time: 193 us -> 168 us (0.87)
  local copies, waits for them, and re-layouts: 52.7 us -> 33.9 us
  blocking collectives: 65.3 us -> 51.1 us
  waiting for transfers between devices: 0.01 us -> 8.09 us
    slice x3, local copies, waits for them, and re-layouts: 23.2 us -> 3.52 us  [per_device(): fields_now[:, height]]
    all_gather x1 -> x0, blocking collectives: 13.6 us -> none  [per_device(): lax.all_gather(own_bottom, 'xg', axis=0, tiled=True)]
    ppermute x0 -> x2, starting transfers between devices: none -> 5.89 us  [_settle_sheets(): ppermute(right_arr, axis_id, [(idx, (idx - f_now) % w_next) for idx in ra...]
    all_to_all x1, waiting for transfers between devices: 0.01 us -> 4.92 us  [per_device(): lax.all_to_all(send_gain, ('atm', 'xg'), split_axis=0, concat_axis=0, til...]
    ppermute x0 -> x2, waiting for transfers between devices: none -> 3.15 us  [_settle_sheets(): ppermute(right_arr, axis_id, [(idx, (idx - f_now) % w_next) for idx in ra...]
    all_to_all x1, starting transfers between devices: 5.35 us -> 2.78 us  [per_device(): lax.all_to_all(send_value, ('atm', 'xg'), split_axis=0, concat_axis=0, ti...]
    unnamed x201 -> x205, local copies, waits for them, and re-layouts: 5.72 us -> 5.51 us
  transfers between devices with their start and end apart: 3 -> 5, of which waited for: 0 -> 2; matrix products, arithmetic and copies ran while one was open for 26% -> 19% of each run, Pallas kernels for 0% -> 0%
where the time goes in v1:
time: 168 us; the launch traced here: 167 us
  blocking collectives  51.1 us (30%)
  matrix products  42.8 us (25%)
  local copies, waits for them, and re-layouts  33.9 us (20%)
  starting transfers between devices  17.3 us (10%)
  other arithmetic  10.7 us (6%)
  waiting for transfers between devices  8.09 us (5%)
  between operations  3.37 us (2%)
    all_gather x1, blocking collectives, per_device(): lax.all_gather(own_carry, 'xg', axis=0, tiled=True)  21.2 us
    dot_general x1, matrix products, per_device(): jnp.einsum('kxb,kfb->kfx', weight, value_slots, precision=HIGHEST)  16.4 us
    all_gather x1, blocking collectives, per_device(): lax.all_gather(own_multiplier, 'xg', axis=0, tiled=True)  15.1 us
    all_gather x1, blocking collectives, per_device(): lax.all_gather(own_inverse, 'xg', axis=0, tiled=True)  14.7 us
    dot_general x1, matrix products, per_device(): gain_part = jnp.einsum('kxb,kb->kx', weight, gain_slots, precision=HIGHEST)  11.8 us
    dot_general x1, matrix products, per_device(): jnp.einsum('kxb,kfx->kfb', weight, surface_flux[margin_block[0]], precisi...  7.85 us
    ppermute x2, starting transfers between devices, _settle_sheets(): ppermute(right_arr, axis_id, [(idx, (idx - f_now) % w_next) for idx in ra...  5.89 us
    all_to_all x1, starting transfers between devices, per_device(): lax.all_to_all(reply.reshape(atm_count * xg_count, pair_slots, field_shar...  5.65 us
  transfers between devices with their start and end apart: 5, of which 2 were waited for; matrix products, arithmetic and copies ran while one was open for 19% of the time, Pallas kernels for 0%

profile of v1, /device:TPU:0, one launch (start us, length us, event | category | flops | bytes accessed | tf_op | source)
XLA Modules:
  0.0 167.2 jit_solution(4685497540422186497)
XLA Ops:
  0.6 1.0 fusion.216
  1.7 1.2 fusion.212
  2.9 1.2 fusion.215
  4.1 1.2 fusion.217
  5.3 1.4 fusion.213
  6.7 1.2 fusion.214
  8.0 1.3 fusion.176
  9.3 5.1 %collective-permute-start = (f32[4,128]{1,0:T(4,128)S(1)}, f32[4,128]{1,0:T(4,128)S(1)}, u32[]{:S(2)}, u32[]{:S(2)}) collective-permute-start(f32[4,128]{1,0:T(4,128)S(1)} %get-tuple-element.36), channel_id=1, source_target_pairs={{0,3},{1,0},{2,1},{3,2},{4,7},{5,4},{6,5},{7,6},{8,11},{9,8},{10,9... | collective-permute-start | bytes 6152 | tf_op jit(solution)/shard_map/ppermute | solution.py:20
  14.4 0.7 fusion.172
  16.7 15.1 %all_gather.10 = f32[16,48,128]{2,1,0:T(8,128)S(1)} all-gather(f32[4,48,128]{2,1,0:T(8,128)S(1)} %copy.726), channel_id=1, replica_groups=mesh['atm'=8,'xg'=4] {'xg'}, dimensions={0}, use_global_device_ids=true | all-gather | bytes 491520 | tf_op jit(solution)/shard_map/all_gather | solution.py:69
  32.1 0.7 fusion.209
  32.9 14.7 %all_gather.9 = f32[16,48,128]{2,1,0:T(8,128)S(1)} all-gather(f32[4,48,128]{2,1,0:T(8,128)S(1)} %copy.724), channel_id=1, replica_groups=mesh['atm'=8,'xg'=4] {'xg'}, dimensions={0}, use_global_device_ids=true | all-gather | bytes 491520 | tf_op jit(solution)/shard_map/all_gather | solution.py:68
  47.6 0.7 fusion.210
  48.3 0.7 fusion.206
  49.0 0.7 fusion.208
  49.8 0.7 fusion.202
  50.5 1.4 fusion.200
  52.0 1.4 fusion.201
  54.1 2.7 %fusion.22 = (f32[16,13,128]{2,0,1:T(8,128)S(1)}, f32[16,13,128]{2,0,1:T(8,128)S(1)}, f32[16,13,128]{2,0,1:T(8,128)S(1)}, f32[16,13,128]{2,0,1:T(8,128)}, f32[16...) fusion(f32[16,1,13,128]{3,1,2,0:T(1,128)S(1)} %get-tuple-elemen, ...), kind=kLoop, calls=%fused_computation.217 | loop fusion | flops 3807232 | bytes 8454144 | tf_op jit(solution)/shard_map/add | solution.py:81
  57.3 0.8 collective-permute-start.1
  58.7 3.2 %collective-permute-done.1 = f32[8,128]{1,0:T(8,128)S(1)} collective-permute-done((f32[8,128]{1,0:T(8,128)S(1)}, f32[8,128]{1,0:T(8,128)S(1)}, u32[]{:S(2)}, u32[]{:S(2)}) %collective-permute-start.1) | collective-permute-done | bytes 4128 | tf_op jit(solution)/shard_map/ppermute | solution.py:20
  62.0 1.2 gather_fusion.2
  63.2 2.9 %all-to-all-start.1 = ((f32[32,2,32]{2,1,0:T(2,128)}), f32[32,2,32]{2,1,0:T(2,128)S(1)}, u32[]{:S(2)}, u32[]{:S(2)}) async-start(f32[32,2,32]{2,1,0:T(2,128)} %bitcast.345), calls=%async_computation.1 | async-start | bytes 65536 | tf_op jit(solution)/shard_map/all_to_all | solution.py:95
  67.5 1.0 copy.777
  68.5 4.9 %all-to-all-done.1 = f32[32,2,32]{2,1,0:T(2,128)S(1)} async-done(((f32[32,2,32]{2,1,0:T(2,128)}), f32[32,2,32]{2,1,0:T(2,128)S(1)}, u32[]{:S(2)}, u32[]{:S(2)}) %all-to-all-start.1) | async-done | bytes 8224 | tf_op jit(solution)/shard_map/all_to_all | solution.py:95
  73.4 2.8 %all-to-all-start = ((f32[32,2,13,128]{3,1,2,0:T(2,128)}), f32[32,2,13,128]{3,1,2,0:T(2,128)S(1)}, u32[]{:S(2)}, u32[]{:S(2)}) async-start(f32[32,2,13,128]{3,1,2,0:T(2,128)} %copy.777), calls=%async_computation | async-start | bytes 851968 | tf_op jit(solution)/shard_map/all_to_all | solution.py:94
  76.7 1.2 gather_fusion.3
  78.1 11.8 %fusion.2 = f32[96,1,128]{2,1,0:T(1,128)S(1)} fusion(f32[96,128,1]{1,2,0:T(1,128)S(1)} %copy.792, f32[1,96,128,128]{3,2,1,0:T(8,128)} %param.21), kind=kOutput, calls=%fused_computation.7 | convolution fusion | flops 18874368 | bytes 6389760 | tf_op jit(solution)/shard_map/kxb,kb->kx/dot_general | solution.py:114
  90.3 2.8 %gather_fusion.1 = f32[96,4,13,128]{3,1,2,0:T(4,128)S(1)} fusion(f32[8,4,2,13,128]{4,1,3,2,0:T(4,128)S(1)} %copy.779, s32[96]{0:T(128)S(1)} %fusion.172), kind=kCustom, calls=%fused_computation.1 | custom fusion | bytes 5112576 | tf_op jit(solution)/shard_map/gather | solution.py:104
  93.4 16.4 %fusion.4 = f32[96,52,128]{2,1,0:T(8,128)S(1)} fusion(f32[1,96,128,128]{3,2,1,0:T(8,128)} %param.21, f32[96,52,128]{2,0,1:T(8,128)S(1)} %bitcast.1159), kind=kOutput, calls=%fused_computation.9 | convolution fusion | flops 981467136 | bytes 11403264 | tf_op jit(solution)/shard_map/kxb,kfb->kfx/dot_general | solution.py:113
  109.8 1.6 fusion.15
  112.2 0.8 gather_fusion.4
  113.0 7.9 %fusion = f32[96,52,128]{2,1,0:T(8,128)S(1)} fusion(f32[96,52,128]{2,1,0:T(8,128)S(1)} %gather_fusion.4, f32[1,96,128,128]{3,2,1,0:T(8,128)} %param.21), kind=kOutput, calls=%fused_computation.5 | convolution fusion | flops 981467136 | bytes 11403264 | tf_op jit(solution)/shard_map/kxb,kfx->kfb/dot_general | solution.py:124
  121.6 1.5 convolution_bitcast_fusion
  123.2 1.1 copy.789
  124.3 5.7 %all-to-all-start.2 = ((f32[32,2,13,128]{3,1,2,0:T(2,128)}), f32[32,2,13,128]{3,1,2,0:T(2,128)S(1)}, u32[]{:S(2)}, u32[]{:S(2)}) async-start(f32[32,2,13,128]{3,1,2,0:T(2,128)} %copy.789), calls=%async_computation.2 | async-start | bytes 851968 | tf_op jit(solution)/shard_map/all_to_all | solution.py:131
  130.0 21.2 %all_gather.11 = f32[16,48,128]{2,1,0:T(8,128)S(1)} all-gather(f32[4,48,128]{2,1,0:T(8,128)} %copy.727), channel_id=1, replica_groups=mesh['atm'=8,'xg'=4] {'xg'}, dimensions={0}, use_global_device_ids=true | all-gather | bytes 491520 | tf_op jit(solution)/shard_map/all_gather | solution.py:70
  151.2 0.7 fusion.205
  151.9 0.8 fusion.204
  152.7 0.7 fusion.203
  153.4 1.3 constant_dynamic-slice_fusion
  155.1 3.5 %constant_dynamic-update-slice_fusion.191 = (f32[16,48,13,128]{3,0,2,1:T(8,128)S(1)}, f32[16,13,128]{2,0,1:T(8,128)S(1)}, f32[16,13,128]{2,0,1:T(8,128)S(1)}, f3...) fusion(f32[16,1,13,128]{3,1,2,0:T(1,128)} %copy-done.33, ...), kind=kOutput, calls=%fused_computation.214 | convolution fusion | flops 24894464 | bytes 8986880 | tf_op jit(solution)/shard_map/rdp,dpfb->rfb/dot_general | solution.py:141
  158.7 0.8 constant_dynamic-update-slice_fusion.190
  159.4 0.7 constant_dynamic-update-slice_fusion.188
  160.2 0.7 constant_dynamic-update-slice_fusion.186
  160.9 0.7 constant_dynamic-update-slice_fusion.184
  161.7 0.7 constant_dynamic-update-slice_fusion.182
  163.3 3.9 %copy.791 = f32[16,48,13,128]{3,1,2,0:T(8,128)} copy(f32[16,48,13,128]{3,0,2,1:T(8,128)S(1)} %constant_dynamic-update-slice_fusion.144) | data formatting | bytes 10223616
  (304 shorter events, 7.4 us)
Async XLA Ops:
  0.6 49.1 %copy-start = (f32[16,48,13,128]{3,1,2,0:T(8,128)S(1)}, f32[16,48,13,128]{3,1,2,0:T(8,128)}, u32[]{:S(2)}) copy-start(f32[16,48,13,128]{3,1,2,0:T(8,128)} %param.13) | copy-start | bytes 15335428
  9.3 48.0 %collective-permute-start = (f32[4,128]{1,0:T(4,128)S(1)}, f32[4,128]{1,0:T(4,128)S(1)}, u32[]{:S(2)}, u32[]{:S(2)}) collective-permute-start(f32[4,128]{1,0:T(4,128)S(1)} %get-tuple-element.36), channel_id=1, source_target_pairs={{0,3},{1,0},{2,1},{3,2},{4,7},{5,4},{6,5},{7,6},{8,11},{9,8},{10,9... | collective-permute-start | bytes 6152 | tf_op jit(solution)/shard_map/ppermute | solution.py:20
  31.9 21.7 %copy-start.68 = (f32[16,1,128]{2,1,0:T(1,128)}, f32[16,1,128]{2,1,0:T(1,128)S(1)}, u32[]{:S(2)}) copy-start(f32[16,1,128]{2,1,0:T(1,128)S(1)} %get-tuple-element.318) | copy-start | bytes 24580
  31.9 21.7 %copy-start.69 = (f32[16,1,128]{2,1,0:T(1,128)}, f32[16,1,128]{2,1,0:T(1,128)S(1)}, u32[]{:S(2)}) copy-start(f32[16,1,128]{2,1,0:T(1,128)S(1)} %get-tuple-element.320) | copy-start | bytes 24580
  31.9 21.7 %copy-start.70 = (f32[16,1,128]{2,1,0:T(1,128)}, f32[16,1,128]{2,1,0:T(1,128)S(1)}, u32[]{:S(2)}) copy-start(f32[16,1,128]{2,1,0:T(1,128)S(1)} %get-tuple-element.322) | copy-start | bytes 24580
  31.9 21.7 %copy-start.71 = (f32[16,1,128]{2,1,0:T(1,128)}, f32[16,1,128]{2,1,0:T(1,128)S(1)}, u32[]{:S(2)}) copy-start(f32[16,1,128]{2,1,0:T(1,128)S(1)} %get-tuple-element.324) | copy-start | bytes 24580
  31.9 21.7 %copy-start.72 = (f32[16,1,128]{2,1,0:T(1,128)}, f32[16,1,128]{2,1,0:T(1,128)S(1)}, u32[]{:S(2)}) copy-start(f32[16,1,128]{2,1,0:T(1,128)S(1)} %get-tuple-element.326) | copy-start | bytes 24580
  31.9 21.7 %copy-start.73 = (f32[16,1,128]{2,1,0:T(1,128)}, f32[16,1,128]{2,1,0:T(1,128)S(1)}, u32[]{:S(2)}) copy-start(f32[16,1,128]{2,1,0:T(1,128)S(1)} %get-tuple-element.327) | copy-start | bytes 24580
  32.0 21.6 %copy-start.74 = (f32[16,1,128]{2,1,0:T(1,128)}, f32[16,1,128]{2,1,0:T(1,128)S(1)}, u32[]{:S(2)}) copy-start(f32[16,1,128]{2,1,0:T(1,128)S(1)} %get-tuple-element.253) | copy-start | bytes 24580
  32.1 21.6 %copy-start.75 = (f32[16,1,128]{2,1,0:T(1,128)}, f32[16,1,128]{2,1,0:T(1,128)S(1)}, u32[]{:S(2)}) copy-start(f32[16,1,128]{2,1,0:T(1,128)S(1)} %get-tuple-element.255) | copy-start | bytes 24580
  32.1 21.6 %copy-start.76 = (f32[16,1,128]{2,1,0:T(1,128)}, f32[16,1,128]{2,1,0:T(1,128)S(1)}, u32[]{:S(2)}) copy-start(f32[16,1,128]{2,1,0:T(1,128)S(1)} %get-tuple-element.257) | copy-start | bytes 24580
  32.1 21.6 %copy-start.77 = (f32[16,1,128]{2,1,0:T(1,128)}, f32[16,1,128]{2,1,0:T(1,128)S(1)}, u32[]{:S(2)}) copy-start(f32[16,1,128]{2,1,0:T(1,128)S(1)} %get-tuple-element.259) | copy-start | bytes 24580
  32.1 21.6 %copy-start.78 = (f32[16,1,128]{2,1,0:T(1,128)}, f32[16,1,128]{2,1,0:T(1,128)S(1)}, u32[]{:S(2)}) copy-start(f32[16,1,128]{2,1,0:T(1,128)S(1)} %get-tuple-element.261) | copy-start | bytes 24580
  32.1 21.6 %copy-start.79 = (f32[16,1,128]{2,1,0:T(1,128)}, f32[16,1,128]{2,1,0:T(1,128)S(1)}, u32[]{:S(2)}) copy-start(f32[16,1,128]{2,1,0:T(1,128)S(1)} %get-tuple-element.263) | copy-start | bytes 24580
  32.1 21.6 %copy-start.80 = (f32[16,1,128]{2,1,0:T(1,128)}, f32[16,1,128]{2,1,0:T(1,128)S(1)}, u32[]{:S(2)}) copy-start(f32[16,1,128]{2,1,0:T(1,128)S(1)} %get-tuple-element.265) | copy-start | bytes 24580
  57.3 4.6 %collective-permute-start.1 = (f32[8,128]{1,0:T(8,128)S(1)}, f32[8,128]{1,0:T(8,128)S(1)}, u32[]{:S(2)}, u32[]{:S(2)}) collective-permute-start(f32[8,128]{1,0:T(8,128)S(1)} %pad_maximum_fusion), channel_id=1, source_target_pairs={{0,2},{1,3},{2,0},{3,1},{4,6},{5,7},{6,4},{7,5},{8,10},{9,11},{10,... | collective-permute-start | bytes 12296 | tf_op jit(solution)/shard_map/ppermute | solution.py:20
  63.2 10.2 %all-to-all-start.1 = ((f32[32,2,32]{2,1,0:T(2,128)}), f32[32,2,32]{2,1,0:T(2,128)S(1)}, u32[]{:S(2)}, u32[]{:S(2)}) async-start(f32[32,2,32]{2,1,0:T(2,128)} %bitcast.345), calls=%async_computation.1 | async-start | bytes 65536 | tf_op jit(solution)/shard_map/all_to_all | solution.py:95
  66.8 23.1 %copy-start.84 = (f32[16,128]{1,0:T(8,128)S(1)}, f32[16,128]{1,0:T(8,128)}, u32[]{:S(2)}) copy-start(f32[16,128]{1,0:T(8,128)} %param.23) | copy-start | bytes 24580
  66.9 23.1 %copy-start.85 = (f32[16,128]{1,0:T(8,128)S(1)}, f32[16,128]{1,0:T(8,128)}, u32[]{:S(2)}) copy-start(f32[16,128]{1,0:T(8,128)} %param.25) | copy-start | bytes 24580
  66.9 23.1 %copy-start.86 = (s32[16,128]{1,0:T(8,128)S(1)}, s32[16,128]{1,0:T(8,128)}, u32[]{:S(2)}) copy-start(s32[16,128]{1,0:T(8,128)} %param.24) | copy-start | bytes 24580
  73.4 16.7 %all-to-all-start = ((f32[32,2,13,128]{3,1,2,0:T(2,128)}), f32[32,2,13,128]{3,1,2,0:T(2,128)S(1)}, u32[]{:S(2)}, u32[]{:S(2)}) async-start(f32[32,2,13,128]{3,1,2,0:T(2,128)} %copy.777), calls=%async_computation | async-start | bytes 851968 | tf_op jit(solution)/shard_map/all_to_all | solution.py:94
  120.8 33.9 %copy-start.2 = (f32[16,13,128]{2,0,1:T(8,128)S(1)}, f32[16,13,128]{2,0,1:T(8,128)}, u32[]{:S(2)}) copy-start(f32[16,13,128]{2,0,1:T(8,128)} %get-tuple-element.56) | copy-start | bytes 319492
  120.9 33.9 %copy-start.3 = (f32[16,13,128]{2,0,1:T(8,128)S(1)}, f32[16,13,128]{2,0,1:T(8,128)}, u32[]{:S(2)}) copy-start(f32[16,13,128]{2,0,1:T(8,128)} %get-tuple-element.57) | copy-start | bytes 319492
  120.9 33.9 %copy-start.4 = (f32[16,13,128]{2,0,1:T(8,128)S(1)}, f32[16,13,128]{2,0,1:T(8,128)}, u32[]{:S(2)}) copy-start(f32[16,13,128]{2,0,1:T(8,128)} %get-tuple-element.58) | copy-start | bytes 319492
  120.9 33.9 %copy-start.5 = (f32[16,13,128]{2,0,1:T(8,128)S(1)}, f32[16,13,128]{2,0,1:T(8,128)}, u32[]{:S(2)}) copy-start(f32[16,13,128]{2,0,1:T(8,128)} %get-tuple-element.59) | copy-start | bytes 319492
  120.9 33.9 %copy-start.6 = (f32[16,13,128]{2,0,1:T(8,128)S(1)}, f32[16,13,128]{2,0,1:T(8,128)}, u32[]{:S(2)}) copy-start(f32[16,13,128]{2,0,1:T(8,128)} %get-tuple-element.60) | copy-start | bytes 319492
  120.9 33.9 %copy-start.7 = (f32[16,13,128]{2,0,1:T(8,128)S(1)}, f32[16,13,128]{2,0,1:T(8,128)}, u32[]{:S(2)}) copy-start(f32[16,13,128]{2,0,1:T(8,128)} %get-tuple-element.61) | copy-start | bytes 319492
  120.9 33.9 %copy-start.8 = (f32[16,13,128]{2,0,1:T(8,128)S(1)}, f32[16,13,128]{2,0,1:T(8,128)}, u32[]{:S(2)}) copy-start(f32[16,13,128]{2,0,1:T(8,128)} %get-tuple-element.62) | copy-start | bytes 319492
  120.9 33.9 %copy-start.9 = (f32[16,13,128]{2,0,1:T(8,128)S(1)}, f32[16,13,128]{2,0,1:T(8,128)}, u32[]{:S(2)}) copy-start(f32[16,13,128]{2,0,1:T(8,128)} %get-tuple-element.63) | copy-start | bytes 319492
  120.9 33.9 %copy-start.10 = (f32[16,13,128]{2,0,1:T(8,128)S(1)}, f32[16,13,128]{2,0,1:T(8,128)}, u32[]{:S(2)}) copy-start(f32[16,13,128]{2,0,1:T(8,128)} %get-tuple-element.64) | copy-start | bytes 319492
  120.9 33.9 %copy-start.11 = (f32[16,13,128]{2,0,1:T(8,128)S(1)}, f32[16,13,128]{2,0,1:T(8,128)}, u32[]{:S(2)}) copy-start(f32[16,13,128]{2,0,1:T(8,128)} %get-tuple-element.65) | copy-start | bytes 319492
  120.9 33.9 %copy-start.12 = (f32[16,13,128]{2,0,1:T(8,128)S(1)}, f32[16,13,128]{2,0,1:T(8,128)}, u32[]{:S(2)}) copy-start(f32[16,13,128]{2,0,1:T(8,128)} %get-tuple-element.66) | copy-start | bytes 319492
  121.0 33.9 %copy-start.13 = (f32[16,13,128]{2,0,1:T(8,128)S(1)}, f32[16,13,128]{2,0,1:T(8,128)}, u32[]{:S(2)}) copy-start(f32[16,13,128]{2,0,1:T(8,128)} %get-tuple-element.67) | copy-start | bytes 319492
  121.0 33.9 %copy-start.14 = (f32[16,13,128]{2,0,1:T(8,128)S(1)}, f32[16,13,128]{2,0,1:T(8,128)}, u32[]{:S(2)}) copy-start(f32[16,13,128]{2,0,1:T(8,128)} %get-tuple-element.68) | copy-start | bytes 319492
  121.0 33.9 %copy-start.15 = (f32[16,13,128]{2,0,1:T(8,128)S(1)}, f32[16,13,128]{2,0,1:T(8,128)}, u32[]{:S(2)}) copy-start(f32[16,13,128]{2,0,1:T(8,128)} %get-tuple-element.69) | copy-start | bytes 319492
  121.0 33.9 %copy-start.16 = (f32[16,13,128]{2,0,1:T(8,128)S(1)}, f32[16,13,128]{2,0,1:T(8,128)}, u32[]{:S(2)}) copy-start(f32[16,13,128]{2,0,1:T(8,128)} %get-tuple-element.70) | copy-start | bytes 319492
  121.0 33.9 %copy-start.17 = (f32[16,13,128]{2,0,1:T(8,128)S(1)}, f32[16,13,128]{2,0,1:T(8,128)}, u32[]{:S(2)}) copy-start(f32[16,13,128]{2,0,1:T(8,128)} %get-tuple-element.71) | copy-start | bytes 319492
  121.0 33.9 %copy-start.18 = (f32[16,13,128]{2,0,1:T(8,128)S(1)}, f32[16,13,128]{2,0,1:T(8,128)}, u32[]{:S(2)}) copy-start(f32[16,13,128]{2,0,1:T(8,128)} %get-tuple-element.72) | copy-start | bytes 319492
  121.0 33.9 %copy-start.19 = (f32[16,13,128]{2,0,1:T(8,128)S(1)}, f32[16,13,128]{2,0,1:T(8,128)}, u32[]{:S(2)}) copy-start(f32[16,13,128]{2,0,1:T(8,128)} %get-tuple-element.73) | copy-start | bytes 319492
  121.0 33.9 %copy-start.20 = (f32[16,13,128]{2,0,1:T(8,128)S(1)}, f32[16,13,128]{2,0,1:T(8,128)}, u32[]{:S(2)}) copy-start(f32[16,13,128]{2,0,1:T(8,128)} %get-tuple-element.74) | copy-start | bytes 319492
  121.0 33.9 %copy-start.21 = (f32[16,13,128]{2,0,1:T(8,128)S(1)}, f32[16,13,128]{2,0,1:T(8,128)}, u32[]{:S(2)}) copy-start(f32[16,13,128]{2,0,1:T(8,128)} %get-tuple-element.75) | copy-start | bytes 319492
  121.0 33.9 %copy-start.22 = (f32[16,13,128]{2,0,1:T(8,128)S(1)}, f32[16,13,128]{2,0,1:T(8,128)}, u32[]{:S(2)}) copy-start(f32[16,13,128]{2,0,1:T(8,128)} %get-tuple-element.76) | copy-start | bytes 319492
  121.1 33.9 %copy-start.24 = (f32[16,1,13,128]{3,1,2,0:T(1,128)S(1)}, f32[16,1,13,128]{3,1,2,0:T(1,128)}, u32[]{:S(2)}) copy-start(f32[16,1,13,128]{3,1,2,0:T(1,128)} %copy-done.23) | copy-start | bytes 319492
  121.1 33.9 %copy-start.26 = (f32[16,1,13,128]{3,1,2,0:T(1,128)S(1)}, f32[16,1,13,128]{3,1,2,0:T(1,128)}, u32[]{:S(2)}) copy-start(f32[16,1,13,128]{3,1,2,0:T(1,128)} %copy-done.25) | copy-start | bytes 319492
  121.1 33.9 %copy-start.28 = (f32[16,1,13,128]{3,1,2,0:T(1,128)S(1)}, f32[16,1,13,128]{3,1,2,0:T(1,128)}, u32[]{:S(2)}) copy-start(f32[16,1,13,128]{3,1,2,0:T(1,128)} %copy-done.27) | copy-start | bytes 319492
  121.1 33.9 %copy-start.30 = (f32[16,1,13,128]{3,1,2,0:T(1,128)S(1)}, f32[16,1,13,128]{3,1,2,0:T(1,128)}, u32[]{:S(2)}) copy-start(f32[16,1,13,128]{3,1,2,0:T(1,128)} %copy-done.29) | copy-start | bytes 319492
  121.1 33.9 %copy-start.32 = (f32[16,1,13,128]{3,1,2,0:T(1,128)S(1)}, f32[16,1,13,128]{3,1,2,0:T(1,128)}, u32[]{:S(2)}) copy-start(f32[16,1,13,128]{3,1,2,0:T(1,128)} %copy-done.31) | copy-start | bytes 319492
  124.3 30.4 %all-to-all-start.2 = ((f32[32,2,13,128]{3,1,2,0:T(2,128)}), f32[32,2,13,128]{3,1,2,0:T(2,128)S(1)}, u32[]{:S(2)}, u32[]{:S(2)}) async-start(f32[32,2,13,128]{3,1,2,0:T(2,128)} %copy.789), calls=%async_computation.2 | async-start | bytes 851968 | tf_op jit(solution)/shard_map/all_to_all | solution.py:131
  (47 other events, 264.6 us)
